TPU v7x, 256 devices: a whole 4x4x8 slice. The times are simulated.
256 devices in a mesh: row: 32 (over z, x), col: 8 (over y, core).
Axes of the slice: x: 4, y: 4, z: 8, core: 2. Of those that a mesh axis runs over, the one named last changes fastest.
Arguments:
- right_side: float32 [15, 512, 512], P(None, 'row'), may hold values from -6 to 6
- off_blocks: float32 [8, 512, 2176], P('col', 'row'), may hold values from -0.09375 to 0.09375
- diag_inverse: float32 [8, 512, 960], P('col', 'row'), as said below
Outputs:
- forward_solution: float32 [8, 960, 512], P('col')
- solution: float32 [8, 4, 512, 512], P('col', None, 'row')
Inputs may be any that keep to these rules, and one draw needn't show every extreme that they name: `diag_inverse`: read through the block map of the first step, each block D(n) is lower triangular with a positive diagonal between 0.5 and 2.
All inputs are finite; a program needn't handle non-finite values.
Results may differ from a plain program's by a relative error of at most 0.00011.
Values sent between devices are 32-bit elements; how exact they have to be, the bound alone decides.
No kernel may reach another device: no remote copies, remote signals or barrier semaphores. Data moves between devices by JAX's collectives and lax.ppermute only.
A program may use at most 64 MiB of HBM per device.

v0:
```python
import jax
import jax.numpy as jnp
from jax import lax
from jax.sharding import PartitionSpec as P

W = 512
LEVELS = 4


def swapped(value, axis, apart):
    mask = 2**apart
    pairs = [(source, source ^ mask) for source in range(lax.axis_size(axis))]
    return lax.ppermute(value, axis, pairs)


def pair_start(depth_down, depth_up):
    return (depth_down - 2) * 2**depth_down + 2 + depth_up * 2**depth_down


def group_sum(values, bit_count):
    for bit_num in range(bit_count):
        values = values + swapped(values, "col", bit_num)
    return values


def solve_block(right_side, off_blocks, diag_inverse):
    highest = lax.Precision.HIGHEST
    col_count = lax.axis_size("col")
    column = lax.axis_index("col")
    totals = [None] * LEVELS
    forward = [None] * LEVELS
    for depth_now in reversed(range(LEVELS)):
        group = col_count >> depth_now
        width = W // group
        bit_count = group.bit_length() - 1
        node_index = 2**depth_now - 1 + column // group
        residue = lax.dynamic_index_in_dim(right_side, node_index, 0, keepdims=False)
        if totals[depth_now] is not None:
            residue = residue - group_sum(totals[depth_now], bit_count)
        start = (2**depth_now - 1) * W // col_count
        inverse = diag_inverse[0, :, start : start + width]
        partial_value = jnp.einsum(
            "ba,br->ar", inverse, residue, precision=highest, preferred_element_type=jnp.float32
        )
        solved = lax.psum(partial_value, "row")
        forward[depth_now] = solved
        for depth_up in range(depth_now):
            begin = pair_start(depth_now, depth_up) * W // col_count
            block = off_blocks[0, :, begin : begin + width]
            term = jnp.dot(block, solved, precision=highest, preferred_element_type=jnp.float32)
            totals[depth_up] = term if totals[depth_up] is None else totals[depth_up] + term
    totals_down = [None] * LEVELS
    backward = [None] * LEVELS
    for depth_now in range(LEVELS):
        group = col_count >> depth_now
        width = W // group
        bit_count = group.bit_length() - 1
        residue = forward[depth_now]
        if totals_down[depth_now] is not None:
            residue = residue - lax.psum(totals_down[depth_now], "row")
        start = (2**depth_now - 1) * W // col_count
        inverse = diag_inverse[0, :, start : start + width]
        partial_value = jnp.dot(
            inverse, residue, precision=highest, preferred_element_type=jnp.float32
        )
        solved = group_sum(partial_value, bit_count)
        backward[depth_now] = solved
        for depth_down in range(depth_now + 1, LEVELS):
            width_down = W // (col_count >> depth_down)
            begin = pair_start(depth_down, depth_now) * W // col_count
            block = off_blocks[0, :, begin : begin + width_down]
            term = jnp.einsum(
                "ij,ir->jr", block, solved, precision=highest, preferred_element_type=jnp.float32
            )
            totals_down[depth_down] = (
                term if totals_down[depth_down] is None else totals_down[depth_down] + term
            )
    return (jnp.concatenate(forward, axis=0)[None], jnp.stack(backward, axis=0)[None])


def per_device(right_side, off_blocks, diag_inverse):
    forward_piece, backward_piece = solve_block(right_side, off_blocks, diag_inverse)
    return (forward_piece, backward_piece)


def solution(mesh):
    return jax.shard_map(
        per_device,
        mesh=mesh,
        in_specs=(P(None, "row", None), P("col", "row", None), P("col", "row", None)),
        out_specs=(P("col", None, None), P("col", None, "row", None)),
        check_vma=False,
    )
```

profile of v0, /device:TPU:8, one launch (start us, length us, event | category | flops | bytes accessed | tf_op | source)
XLA Modules:
  0.0 1091.3 jit_solution(8329834675328494492)
XLA Ops:
  7.2 2.9 convolution_bitcast_fusion
  10.2 154.2 %all-reduce.8.cloned.1.call-done = f32[512,512]{0,1:T(8,128)} async-done(((f32[512,512]{0,1:T(8,128)}), f32[512,512]{0,1:T(8,128)}) %all-reduce.8.cloned.1.call-update) | async-done | bytes 1048592 | tf_op jit(solution)/shard_map/psum | solution.py:45
  164.3 2.3 convolution_bitcast_fusion.8
  166.7 1.2 collective-permute-done
  167.9 2.2 convolution_bitcast_fusion.1
  170.2 144.9 %all-reduce.10.cloned.1.call-done = f32[256,512]{0,1:T(8,128)} async-done(((f32[256,512]{0,1:T(8,128)}), f32[256,512]{0,1:T(8,128)}) %all-reduce.10.cloned.1.call-update) | async-done | bytes 524304 | tf_op jit(solution)/shard_map/psum | solution.py:45
  315.1 1.7 fusion.36
  316.8 1.0 fusion.4
  317.8 1.2 collective-permute-done.1
  319.0 0.5 collective-permute-start.2
  319.6 3.4 collective-permute-done.2
  323.0 2.1 convolution_bitcast_fusion.4
  325.1 0.5 fusion.39
  325.7 1.0 convolution_add_fusion.4
  326.7 139.5 %all-reduce.12.cloned.1.call-done = f32[128,512]{0,1:T(8,128)} async-done(((f32[128,512]{0,1:T(8,128)}), f32[128,512]{0,1:T(8,128)}) %all-reduce.12.cloned.1.call-update) | async-done | bytes 262160 | tf_op jit(solution)/shard_map/psum | solution.py:45
  466.2 1.4 fusion.3
  467.6 1.2 collective-permute-done.3
  468.8 0.5 collective-permute-start.4
  469.4 3.4 collective-permute-done.4
  472.8 2.1 collective-permute-start.5
  474.9 3.3 collective-permute-done.5
  478.2 2.1 convolution_bitcast_fusion.3
  480.3 141.1 %all-reduce.14.cloned.1.call-done = f32[64,512]{0,1:T(8,128)} async-done(((f32[64,512]{0,1:T(8,128)}), f32[64,512]{0,1:T(8,128)}) %all-reduce.14.cloned.1.call-update) | async-done | bytes 131088 | tf_op jit(solution)/shard_map/psum | solution.py:45
  621.5 1.3 convolution_bitcast_fusion.7
  622.8 1.2 collective-permute-done.6
  624.0 0.5 collective-permute-start.7
  624.6 3.4 collective-permute-done.7
  628.0 2.1 collective-permute-start.8
  630.1 3.3 collective-permute-done.8
  633.4 1.3 convolution_bitcast_fusion.2
  634.7 0.2 all-reduce.18.cloned.1.call-start
  634.9 141.0 %all-reduce.16.cloned.1.call-done = f32[128,512]{0,1:T(8,128)} async-done(((f32[128,512]{0,1:T(8,128)}), f32[128,512]{0,1:T(8,128)}) %all-reduce.16.cloned.1.call-update) | async-done | bytes 262160 | tf_op jit(solution)/shard_map/psum | solution.py:60
  775.9 1.3 convolution_bitcast_fusion.6
  777.3 1.2 collective-permute-done.9
  778.5 0.5 collective-permute-start.10
  779.0 3.4 collective-permute-done.10
  782.4 0.6 fusion.34
  783.0 1.4 fusion.2
  784.5 144.5 %all-reduce.18.cloned.1.call-done = f32[256,512]{0,1:T(8,128)} async-done(((f32[256,512]{0,1:T(8,128)}), f32[256,512]{0,1:T(8,128)}) %all-reduce.18.cloned.1.call-update) | async-done | bytes 524304 | tf_op jit(solution)/shard_map/psum | solution.py:60
  929.0 1.6 convolution_bitcast_fusion.9
  930.7 1.0 fusion.8
  931.9 1.0 fusion.11
  932.9 2.0 fusion.1
  935.0 1.8 maximum_bitcast_fusion
  936.9 1.8 copy.6
  938.7 142.9 %all-reduce.20.cloned.1.call-done = f32[512,512]{0,1:T(8,128)} async-done(((f32[512,512]{0,1:T(8,128)}), f32[512,512]{0,1:T(8,128)}) %all-reduce.20.cloned.1.call-update) | async-done | bytes 1048592 | tf_op jit(solution)/shard_map/psum | solution.py:60
  1081.6 2.2 convolution_bitcast_fusion.5
  1083.8 0.7 maximum_bitcast_fusion.1
  (45 shorter events, 1.1 us)
Async XLA Ops:
  7.2 160.7 %copy-start.4 = (f32[1,16,960]{2,1,0:T(8,128)S(1)}, f32[1,16,960]{2,1,0:T(8,128)}, u32[]{:S(2)}) copy-start(f32[1,16,960]{2,1,0:T(8,128)} %param.5) | copy-start | bytes 184324
  7.2 157.2 %copy-start.3 = (f32[1,16,2176]{2,1,0:T(8,128)S(1)}, f32[1,16,2176]{2,1,0:T(8,128)}, u32[]{:S(2)}) copy-start(f32[1,16,2176]{2,1,0:T(8,128)} %param.4) | copy-start | bytes 417796
  7.2 157.1 %all-reduce.8.cloned.1.call-start = ((), (), s32[]{:S(2)}) async-start(), calls=%async_computation | async-start | bytes 2097152 | tf_op jit(solution)/shard_map/psum | solution.py:45
  10.1 305.0 %all-reduce.10.cloned.1.call-start = ((), (), s32[]{:S(2)}) async-start(), calls=%async_computation.1 | async-start | bytes 1048576 | tf_op jit(solution)/shard_map/psum | solution.py:45
  164.3 152.4 %copy-start = (f32[512,512]{0,1:T(8,128)S(1)}, f32[512,512]{0,1:T(8,128)}, u32[]{:S(2)}) copy-start(f32[512,512]{0,1:T(8,128)} %all-reduce.8.cloned.1.call-done) | copy-start | bytes 3145732
  166.6 1.3 collective-permute-start
  170.1 296.1 %all-reduce.12.cloned.1.call-start = ((), (), s32[]{:S(2)}) async-start(), calls=%async_computation.2 | async-start | bytes 524288 | tf_op jit(solution)/shard_map/psum | solution.py:45
  315.1 10.0 copy-start.1
  317.8 1.3 collective-permute-start.1
  319.0 3.9 collective-permute-start.2
  325.1 296.4 %all-reduce.14.cloned.1.call-start = ((), (), s32[]{:S(2)}) async-start(), calls=%async_computation.3 | async-start | bytes 524288 | tf_op jit(solution)/shard_map/psum | solution.py:45
  466.2 309.7 %copy-start.2 = (f32[128,512]{0,1:T(8,128)S(1)}, f32[128,512]{0,1:T(8,128)}, u32[]{:S(2)}) copy-start(f32[128,512]{0,1:T(8,128)} %all-reduce.12.cloned.1.call-done) | copy-start | bytes 786436
  467.5 1.3 collective-permute-start.3
  468.8 3.9 collective-permute-start.4
  472.8 5.4 collective-permute-start.5
  480.3 295.6 %all-reduce.16.cloned.1.call-start = ((), (), s32[]{:S(2)}) async-start(), calls=%async_computation.4 | async-start | bytes 524288 | tf_op jit(solution)/shard_map/psum | solution.py:60
  622.7 1.3 collective-permute-start.6
  624.0 3.9 collective-permute-start.7
  628.0 5.4 collective-permute-start.8
  634.7 294.3 %all-reduce.18.cloned.1.call-start = ((), (), s32[]{:S(2)}) async-start(), calls=%async_computation.5 | async-start | bytes 1048576 | tf_op jit(solution)/shard_map/psum | solution.py:60
  777.2 1.3 collective-permute-start.9
  778.5 3.9 collective-permute-start.10
  784.5 297.1 %all-reduce.20.cloned.1.call-start = ((), (), s32[]{:S(2)}) async-start(), calls=%async_computation.6 | async-start | bytes 2097152 | tf_op jit(solution)/shard_map/psum | solution.py:60
  930.6 1.3 collective-permute-start.11
  931.9 3.1 copy-start.6
  936.9 1.8 copy-start.7
  936.9 144.7 %copy-start.5 = (f32[1,16,960]{2,1,0:T(8,128)S(1)}, f32[1,16,960]{2,1,0:T(8,128)}, u32[]{:S(2)}) copy-start(f32[1,16,960]{2,1,0:T(8,128)} %param.5) | copy-start | bytes 184324
Sparse Core Ops, SparseCore 0:
  12.0 152.2 all-reduce.7
  170.2 144.8 all-reduce.9
  325.2 140.9 all-reduce.11
  480.4 141.0 all-reduce.13
  634.8 141.0 all-reduce.15
  784.6 144.4 all-reduce.17
  935.1 146.3 all-reduce.19
where the time goes:
time: 1090 us
  waiting for transfers between devices  1030 us (94%)
  matrix products  30.9 us (3%)
  between operations  14.3 us (1%)
    psum x4, waiting for transfers between devices, solve_block(): solved = lax.psum(partial_value, 'row')  580 us
    psum x3, waiting for transfers between devices, solve_block(): residue = residue - lax.psum(totals_down[depth_now], 'row')  428 us
    ppermute x12, waiting for transfers between devices, swapped(): return lax.ppermute(value, axis, pairs)  26.2 us
  transfers between devices with their start and end apart: 19, of which 19 were waited for; matrix products, arithmetic and copies ran while one was open for 1% of the time, Pallas kernels for 0%

commit v1 on v0

--- a/solution.py
+++ b/solution.py
@@ -42,7 +42,7 @@
         partial_value = jnp.einsum(
             "ba,br->ar", inverse, residue, precision=highest, preferred_element_type=jnp.float32
         )
-        solved = lax.psum(partial_value, "row")
+        solved = jnp.sum(lax.all_gather(partial_value, "row"), axis=0)
         forward[depth_now] = solved
         for depth_up in range(depth_now):
             begin = pair_start(depth_now, depth_up) * W // col_count

time: 1090 us -> 1140 us (1.046)
  local copies, waits for them, and re-layouts: 1.8 us -> 56.5 us
  other arithmetic: 2.59 us -> 20.9 us
    psum x4 -> x0, waiting for transfers between devices: 580 us -> none  [solve_block(): solved = lax.psum(partial_value, 'row')]
    all_gather x0 -> x4, waiting for transfers between devices: none -> 563 us  [solve_block(): solved = jnp.sum(lax.all_gather(partial_value, 'row'), axis=0)]
    unnamed x17 -> x8, local copies, waits for them, and re-layouts: 1.8 us -> 56.4 us
    reduce_sum x0 -> x4, other arithmetic: none -> 18.1 us  [solve_block(): solved = jnp.sum(lax.all_gather(partial_value, 'row'), axis=0)]
where the time goes in v1:
time: 1140 us
  waiting for transfers between devices  1020 us (89%)
  local copies, waits for them, and re-layouts  56.5 us (5%)
  matrix products  26 us (2%)
  other arithmetic  20.9 us (2%)
  between operations  14.3 us (1%)
    all_gather x4, waiting for transfers between devices, solve_block(): solved = jnp.sum(lax.all_gather(partial_value, 'row'), axis=0)  563 us
    psum x3, waiting for transfers between devices, solve_block(): residue = residue - lax.psum(totals_down[depth_now], 'row')  427 us
    unnamed x8, local copies, waits for them, and re-layouts  56.4 us
    ppermute x12, waiting for transfers between devices, swapped(): return lax.ppermute(value, axis, pairs)  26.2 us
  transfers between devices with their start and end apart: 19, of which 19 were waited for; matrix products, arithmetic and copies ran while one was open for 1% of the time, Pallas kernels for 0%

profile of v1, /device:TPU:8, one launch (start us, length us, event | category | flops | bytes accessed | tf_op | source)
XLA Modules:
  0.0 1142.2 jit_solution(16321631131346330411)
XLA Ops:
  7.2 2.8 convolution_bitcast_fusion
  10.1 237.2 %all-gather.9.cloned.1.call-done = f32[16384,512]{0,1:T(8,128)} async-done(((f32[512,512]{0,1:T(8,128)}), f32[16384,512]{0,1:T(8,128)}) %all-gather.9.cloned.1.call-update) | async-done | bytes 33554448 | tf_op jit(solution)/shard_map/all_gather | solution.py:45
  247.3 32.5 %copy.8 = f32[64,8,32,512]{3,2,1,0:T(8,128)S(1)} copy(f32[64,8,32,512]{3,1,2,0:T(8,128)} %bitcast.127) | data formatting | bytes 67108864
  279.9 5.4 bitcast_reduce_fusion
  285.2 1.0 convolution_bitcast_fusion.8
  286.3 1.2 collective-permute-done
  287.5 2.2 convolution_bitcast_fusion.1
  289.9 147.7 %all-gather.11.cloned.1.call-done = f32[8192,512]{0,1:T(8,128)} async-done(((f32[256,512]{0,1:T(8,128)}), f32[8192,512]{0,1:T(8,128)}) %all-gather.11.cloned.1.call-update) | async-done | bytes 16777232 | tf_op jit(solution)/shard_map/all_gather | solution.py:45
  437.6 15.8 %copy.9 = f32[64,8,32,256]{3,2,1,0:T(8,128)} copy(f32[64,8,32,256]{3,1,2,0:T(8,128)} %bitcast.128) | data formatting | bytes 33554432
  453.4 8.7 bitcast_reduce_fusion.1
  462.1 0.5 fusion.36
  462.6 1.0 fusion.4
  463.7 1.2 collective-permute-done.1
  465.4 3.4 collective-permute-done.2
  468.8 2.1 convolution_bitcast_fusion.3
  471.2 0.5 fusion.39
  471.7 1.0 convolution_add_fusion.4
  472.7 98.8 %all-gather.13.cloned.1.call-done = f32[4096,512]{0,1:T(8,128)} async-done(((f32[128,512]{0,1:T(8,128)}), f32[4096,512]{0,1:T(8,128)}) %all-gather.13.cloned.1.call-update) | async-done | bytes 8388624 | tf_op jit(solution)/shard_map/all_gather | solution.py:45
  571.6 5.2 copy.10
  576.8 1.6 bitcast_reduce_fusion.2
  578.8 1.2 collective-permute-done.3
  580.5 3.4 collective-permute-done.4
  583.9 2.1 collective-permute-start.5
  586.0 3.3 collective-permute-done.5
  589.3 1.7 convolution_bitcast_fusion.4
  591.1 79.5 %all-gather.15.cloned.1.call-done = f32[2048,512]{1,0:T(8,128)} async-done(((f32[64,512]{1,0:T(8,128)}), f32[2048,512]{1,0:T(8,128)}) %all-gather.15.cloned.1.call-update) | async-done | bytes 4194320 | tf_op jit(solution)/shard_map/all_gather | solution.py:45
  670.6 2.5 reduce_sum.39
  673.4 1.2 collective-permute-done.6
  675.2 3.4 collective-permute-done.7
  678.6 2.1 collective-permute-start.8
  680.7 3.3 collective-permute-done.8
  684.0 1.3 convolution_bitcast_fusion.2
  685.4 141.4 %all-reduce.4.cloned.1.call-done = f32[128,512]{0,1:T(8,128)} async-done(((f32[128,512]{0,1:T(8,128)}), f32[128,512]{0,1:T(8,128)}) %all-reduce.4.cloned.1.call-update) | async-done | bytes 262160 | tf_op jit(solution)/shard_map/psum | solution.py:60
  826.8 1.3 convolution_bitcast_fusion.6
  828.2 1.2 collective-permute-done.9
  829.9 3.4 collective-permute-done.10
  833.3 0.6 fusion.34
  833.9 1.4 fusion.2
  835.7 144.2 %all-reduce.6.cloned.1.call-done = f32[256,512]{0,1:T(8,128)} async-done(((f32[256,512]{0,1:T(8,128)}), f32[256,512]{0,1:T(8,128)}) %all-reduce.6.cloned.1.call-update) | async-done | bytes 524304 | tf_op jit(solution)/shard_map/psum | solution.py:60
  979.9 1.6 convolution_bitcast_fusion.9
  981.6 1.0 fusion.8
  982.8 1.0 fusion.11
  983.8 2.0 fusion.1
  986.0 2.1 maximum_bitcast_fusion
  988.1 2.8 copy.7
  990.9 141.5 %all-reduce.8.cloned.1.call-done = f32[512,512]{0,1:T(8,128)} async-done(((f32[512,512]{0,1:T(8,128)}), f32[512,512]{0,1:T(8,128)}) %all-reduce.8.cloned.1.call-update) | async-done | bytes 1048592 | tf_op jit(solution)/shard_map/psum | solution.py:60
  1132.4 2.2 convolution_bitcast_fusion.5
  1134.7 0.7 maximum_bitcast_fusion.1
  (41 shorter events, 4.5 us)
Async XLA Ops:
  7.2 240.2 %all-gather.9.cloned.1.call-start = ((), (), s32[]{:S(2)}) async-start(), calls=%async_computation.3 | async-start | bytes 34603008 | tf_op jit(solution)/shard_map/all_gather | solution.py:45
  10.1 427.5 %all-gather.11.cloned.1.call-start = ((), (), s32[]{:S(2)}) async-start(), calls=%async_computation.4 | async-start | bytes 17301504 | tf_op jit(solution)/shard_map/all_gather | solution.py:45
  279.8 5.4 copy-start
  279.8 7.6 copy-start.1
  286.2 1.2 collective-permute-start
  289.7 281.9 %all-gather.13.cloned.1.call-start = ((), (), s32[]{:S(2)}) async-start(), calls=%async_computation.5 | async-start | bytes 8650752 | tf_op jit(solution)/shard_map/all_gather | solution.py:45
  463.6 1.3 collective-permute-start.1
  464.9 3.9 collective-permute-start.2
  470.9 199.7 %all-gather.15.cloned.1.call-start = ((), (), s32[]{:S(2)}) async-start(), calls=%async_computation.6 | async-start | bytes 4325376 | tf_op jit(solution)/shard_map/all_gather | solution.py:45
  578.7 1.3 collective-permute-start.3
  580.0 3.9 collective-permute-start.4
  583.9 5.4 collective-permute-start.5
  591.1 235.7 %all-reduce.4.cloned.1.call-start = ((), (), s32[]{:S(2)}) async-start(), calls=%async_computation | async-start | bytes 524288 | tf_op jit(solution)/shard_map/psum | solution.py:60
  673.3 1.3 collective-permute-start.6
  674.6 3.9 collective-permute-start.7
  678.6 5.4 collective-permute-start.8
  685.3 294.6 %all-reduce.6.cloned.1.call-start = ((), (), s32[]{:S(2)}) async-start(), calls=%async_computation.1 | async-start | bytes 1048576 | tf_op jit(solution)/shard_map/psum | solution.py:60
  828.1 1.3 collective-permute-start.9
  829.4 3.9 collective-permute-start.10
  835.4 297.1 %all-reduce.8.cloned.1.call-start = ((), (), s32[]{:S(2)}) async-start(), calls=%async_computation.2 | async-start | bytes 2097152 | tf_op jit(solution)/shard_map/psum | solution.py:60
  981.5 1.3 collective-permute-start.11
Sparse Core Ops, SparseCore 0:
  11.2 236.1 all-gather.8
  289.8 147.7 all-gather.10
  471.0 100.4 all-gather.12
  591.2 79.3 all-gather.14
  685.4 141.3 all-reduce.3
  835.5 144.3 all-reduce.5
  986.0 146.3 all-reduce.7
